TPU v7x, 32 devices: a whole 2x2x4 slice. The times are simulated.
32 devices in a mesh: win: 2 (over x), wide: 8 (over z, y), narrow: 2 (over core).
Axes of the slice: x: 2, y: 2, z: 4, core: 2. Of those that a mesh axis runs over, the one named last changes fastest.
Arguments:
- window_data: float32 [384, 128, 256], P(('win', 'wide'), 'narrow'), parts along dimension 0, may hold values from -6 to 6
- factor_one: float32 [256, 48], P(('win', 'narrow')), parts along dimension 0, may hold values from -0.5 to 0.5
- factor_two: float32 [512, 48], P('win'), parts along dimension 0, may hold values from -0.375 to 0.375
- factor_three: float32 [384, 48], P(('win', 'wide')), parts along dimension 0, may hold values from -0.4375 to 0.4375
Outputs:
- basis_one: float32 [256, 48], P(('win', 'narrow')), parts along dimension 0
- basis_two: float32 [512, 48], P('win'), parts along dimension 0
- basis_three: float32 [384, 48], P(('win', 'wide')), parts along dimension 0
- core_unfolded: float32 [48, 4608], P(None, ('win', 'wide', 'narrow')), parts along dimension 1
There are 2 independent parts, one for each index of `win`. A program takes and returns all parts, laid end to end along the dimension named above; each array names one. Nothing has to cross between parts.
All inputs are finite; a program needn't handle non-finite values.
Results may differ from a plain program's by a relative error of at most 0.0003.
Values sent between devices are 32-bit elements; how exact they have to be, the bound alone decides.
No kernel may reach another device: no remote copies, remote signals or barrier semaphores. Data moves between devices by JAX's collectives and lax.ppermute only.
A program may use at most 64 MiB of HBM per device.

v0:
```python
import jax
import jax.numpy as jnp
from jax import lax
from jax.sharding import PartitionSpec as P

highest = lax.Precision.HIGHEST


def contract(form, left, right):
    return jnp.einsum(form, left, right, precision=highest)


def orthonormal(basis, gram):
    lower = jnp.linalg.cholesky(gram)
    return lax.linalg.triangular_solve(lower, basis, left_side=False, lower=True, transpose_a=True)


def full_core(partial_value):
    flat = partial_value.reshape(
        partial_value.shape[0], partial_value.shape[1] * partial_value.shape[2]
    )
    shares = lax.psum_scatter(flat, ("wide", "narrow"), scatter_dimension=1, tiled=True)
    whole = lax.all_gather(shares, ("wide", "narrow"), axis=1, tiled=True)
    return whole.reshape(partial_value.shape)


def on_device(window_data, factor_one, factor_two, factor_three):
    rank = factor_one.shape[1]
    along_two = contract("kij,jb->kib", window_data, factor_two)
    unfold_part = contract("kib,kc->ibc", along_two, factor_three).reshape(
        along_two.shape[1], rank * rank
    )
    unfold_rows = lax.psum_scatter(unfold_part, "wide", scatter_dimension=1, tiled=True)
    weights_one = lax.psum(jnp.dot(unfold_rows.T, factor_one, precision=highest), "narrow")
    product_one = lax.psum(jnp.dot(unfold_rows, weights_one, precision=highest), "wide")
    gram_one = lax.psum(jnp.dot(product_one.T, product_one, precision=highest), "narrow")
    basis_one = orthonormal(product_one, gram_one)
    along_one = contract("kij,ia->kaj", window_data, basis_one)
    core_two = full_core(
        contract("kab,kc->abc", contract("kaj,jb->kab", along_one, factor_two), factor_three)
    )
    spread_two = contract("abc,kc->kab", core_two, factor_three)
    product_two = lax.psum(contract("kaj,kab->jb", along_one, spread_two), ("wide", "narrow"))
    basis_two = orthonormal(product_two, jnp.dot(product_two.T, product_two, precision=highest))
    along_new = contract("kij,jb->kib", window_data, basis_two)
    unfold_three = contract("kib,ia->kab", along_new, basis_one)
    core_three = full_core(contract("kab,kc->abc", unfold_three, factor_three))
    product_three = lax.psum(contract("kab,abc->kc", unfold_three, core_three), "narrow")
    gram_three = lax.psum(jnp.dot(product_three.T, product_three, precision=highest), "wide")
    basis_three = orthonormal(product_three, gram_three)
    core_part = contract("kab,kc->abc", unfold_three, basis_three).reshape(rank, rank * rank)
    core_shares = lax.psum_scatter(core_part, ("wide", "narrow"), scatter_dimension=1, tiled=True)
    return (basis_one, basis_two, basis_three, core_shares)


def solution(mesh):
    return jax.shard_map(
        on_device,
        mesh=mesh,
        in_specs=(
            P(("win", "wide"), "narrow", None),
            P(("win", "narrow"), None),
            P("win", None),
            P(("win", "wide"), None),
        ),
        out_specs=(
            P(("win", "narrow"), None),
            P("win", None),
            P(("win", "wide"), None),
            P(None, ("win", "wide", "narrow")),
        ),
        check_vma=False,
    )
```

profile of v0, /device:TPU:0, one launch (start us, length us, event | category | flops | bytes accessed | tf_op | source)
XLA Modules:
  0.0 505.6 jit_solution(5925950153966513324)
XLA Ops:
  7.2 0.0 reduce-scatter.11.cloned.1.call-start
  7.2 1.3 copy-done
  8.6 3.1 fusion.12
  11.7 2.2 fusion.3
  13.9 0.0 reduce-scatter.13.cloned.1.call-start
  13.9 67.9 %reduce-scatter.11.cloned.1.call-done = f32[64,288]{0,1:T(8,128)} async-done(((f32[64,2304]{0,1:T(8,128)}), f32[64,288]{0,1:T(8,128)}) %reduce-scatter.11.cloned.1.call-update) | async-done | bytes 73744 | tf_op jit(solution)/shard_map/reduce_scatter | solution.py:33
  81.9 1.2 fusion.34
  83.1 3.5 psum.42
  86.6 1.1 fusion.35
  87.7 34.9 %psum.43 = f32[64,48]{0,1:T(8,128)S(1)} all-reduce(f32[64,48]{0,1:T(8,128)S(1)} %fusion.35), channel_id=1, replica_groups=mesh['win'=2,'wide'=8,'narrow'=2] {'wide'}, use_global_device_ids=true, to_apply=%region_2.0 | all-reduce | flops 3072 | bytes 24576 | tf_op jit(solution)/shard_map/psum | solution.py:35
  122.6 0.2 fusion.36
  122.8 3.4 psum.44
  126.2 0.1 copy.26
  126.3 4.4 cholesky.59
  130.7 0.6 compare_reduce_fusion.2
  131.4 0.7 fusion.14
  132.0 3.7 custom-call.11
  135.7 0.2 fusion.25
  136.0 1.1 convolution_bitcast_fusion
  137.1 1.6 fusion
  138.7 3.1 fusion.31
  141.8 2.7 copy.45
  144.5 0.0 reduce-scatter.15.cloned.1.call-start
  144.6 55.5 %reduce-scatter.13.cloned.1.call-done = f32[144,48]{1,0:T(8,128)} async-done(((f32[2304,48]{1,0:T(8,128)}), f32[144,48]{1,0:T(8,128)}) %reduce-scatter.13.cloned.1.call-update) | async-done | bytes 27664
  200.1 1.0 copy.40
  201.0 21.8 %all-gather = f32[16,144,48]{1,2,0:T(8,128)S(1)} all-gather(f32[1,144,48]{1,2,0:T(8,128)S(1)} %bitcast.116), channel_id=1, replica_groups=mesh['win'=2,'wide'=8,'narrow'=2] {'wide','narrow'}, dimensions={0}, use_global_device_ids=true | all-gather | bytes 470016 | tf_op jit(solution)/shard_map/all_gather | solution.py:23
  222.8 0.5 copy.28
  223.3 1.2 reshape.47
  224.4 2.7 reshape.42
  227.2 4.7 convolution_bitcast_fusion.3
  231.9 1.2 convolution_bitcast_fusion.4
  233.1 57.9 %psum.45 = f32[256,48]{0,1:T(8,128)S(1)} all-reduce(f32[256,48]{0,1:T(8,128)S(1)} %convolution_bitcast_fusion.4), channel_id=1, replica_groups=mesh['win'=2,'wide'=8,'narrow'=2] {'wide','narrow'}, use_global_device_ids=true, to_apply=%region_7.0 | all-reduce | flops 12288 | bytes 98304 | tf_op jit(solution)/shard_map/psum | solution.py:43
  291.0 0.2 fusion.37
  291.2 0.1 copy.30
  291.3 4.4 cholesky.70
  295.7 0.6 compare_reduce_fusion.1
  296.4 0.7 fusion.15
  297.0 3.7 custom-call.12
  300.7 0.2 fusion.20
  301.0 2.3 convolution_bitcast_fusion.2
  303.3 2.1 convolution_bitcast_fusion.1
  305.5 2.0 fusion.7
  307.5 1.5 copy.46
  309.0 0.0 reduce-scatter.17.cloned.1.call-start
  309.1 55.5 %reduce-scatter.15.cloned.1.call-done = f32[144,48]{1,0:T(8,128)} async-done(((f32[2304,48]{1,0:T(8,128)}), f32[144,48]{1,0:T(8,128)}) %reduce-scatter.15.cloned.1.call-update) | async-done | bytes 27664
  364.6 1.0 copy.42
  365.5 21.8 %all-gather.1 = f32[16,144,48]{1,2,0:T(8,128)S(1)} all-gather(f32[1,144,48]{1,2,0:T(8,128)S(1)} %bitcast.117), channel_id=1, replica_groups=mesh['win'=2,'wide'=8,'narrow'=2] {'wide','narrow'}, dimensions={0}, use_global_device_ids=true | all-gather | bytes 470016 | tf_op jit(solution)/shard_map/all_gather | solution.py:23
  387.3 0.5 copy.32
  387.8 1.1 reshape.49
  388.9 1.7 reshape.44
  390.7 1.2 convolution_bitcast_fusion.5
  391.9 3.5 psum.46
  395.4 0.2 fusion.38
  395.6 33.0 %psum.47 = f32[48,48]{0,1:T(8,128)S(1)} all-reduce(f32[48,48]{0,1:T(8,128)S(1)} %fusion.38), channel_id=1, replica_groups=mesh['win'=2,'wide'=8,'narrow'=2] {'wide'}, use_global_device_ids=true, to_apply=%region_10.12 | all-reduce | flops 2304 | bytes 18432 | tf_op jit(solution)/shard_map/psum | solution.py:49
  428.6 0.1 copy.35
  428.7 4.4 cholesky.81
  433.1 0.6 compare_reduce_fusion
  433.8 0.7 fusion.16
  434.4 3.7 custom-call.13
  438.1 0.2 fusion.17
  438.3 2.0 fusion.5
  440.3 1.5 copy.47
  441.9 55.6 %reduce-scatter.17.cloned.1.call-done = f32[144,48]{1,0:T(8,128)} async-done(((f32[2304,48]{1,0:T(8,128)}), f32[144,48]{1,0:T(8,128)}) %reduce-scatter.17.cloned.1.call-update) | async-done | bytes 27664
  497.5 1.6 copy.44
  (25 shorter events, 0.2 us)
Async XLA Ops:
  7.2 1.4 copy-start
  7.2 4.5 copy-start.3
  7.2 74.7 %reduce-scatter.11.cloned.1.call-start = ((), (), s32[]{:S(2)}) async-start(), calls=%async_computation.4 | async-start | bytes 1327104 | tf_op jit(solution)/shard_map/reduce_scatter | solution.py:33
  11.7 70.2 %copy-start.7 = (f32[64,48]{0,1:T(8,128)S(1)}, f32[64,48]{0,1:T(8,128)}, u32[]{:S(2)}) copy-start(f32[64,48]{0,1:T(8,128)} %param.6) | copy-start | bytes 36868
  13.9 186.2 %reduce-scatter.13.cloned.1.call-start = ((), (), s32[]{:S(2)}) async-start(), calls=%async_computation.5 | async-start | bytes 1253376
  135.9 1.1 copy-start.1
  136.0 1.1 copy-start.5
  144.5 220.0 %reduce-scatter.15.cloned.1.call-start = ((), (), s32[]{:S(2)}) async-start(), calls=%async_computation.6 | async-start | bytes 1253376
  297.0 6.3 %copy-start.2 = (f32[64,48]{0,1:T(8,128)S(1)}, f32[64,48]{0,1:T(8,128)}, u32[]{:S(2)}) copy-start(f32[64,48]{0,1:T(8,128)} %copy-done.1) | copy-start | bytes 36868
  301.0 4.5 copy-start.4
  309.0 188.4 %reduce-scatter.17.cloned.1.call-start = ((), (), s32[]{:S(2)}) async-start(), calls=%async_computation.7 | async-start | bytes 1253376
  438.3 3.6 copy-start.6
Sparse Core Ops, SparseCore 0:
  14.0 67.8 reduce-scatter.10
  144.7 55.3 reduce-scatter.12
  309.1 55.3 reduce-scatter.14
  442.0 55.4 reduce-scatter.16
where the time goes:
time: 506 us
  waiting for transfers between devices  235 us (46%)
  blocking collectives  180 us (36%)
  matrix products  30.3 us (6%)
  other arithmetic  28.2 us (6%)
  local copies, waits for them, and re-layouts  18.5 us (4%)
  between operations  14.1 us (3%)
    unnamed x7, waiting for transfers between devices  167 us
    reduce_scatter x1, waiting for transfers between devices, on_device(): lax.psum_scatter(unfold_part, 'wide', scatter_dimension=1, tiled=True)  67.9 us
    psum x1, blocking collectives, on_device(): lax.psum(contract('kaj,kab->jb', along_one, spread_two), ('wide', 'narrow'))  57.9 us
    all_gather x2, blocking collectives, full_core(): whole = lax.all_gather(shares, ('wide', 'narrow'), axis=1, tiled=True)  43.6 us
    psum x1, blocking collectives, on_device(): lax.psum(jnp.dot(unfold_rows, weights_one, precision=highest), 'wide')  34.9 us
    psum x1, blocking collectives, on_device(): lax.psum(jnp.dot(product_three.T, product_three, precision=highest), 'wide')  33 us
    dot_general x12, matrix products, contract(): return jnp.einsum(form, left, right, precision=highest)  26.7 us
    another operation x9, other arithmetic, orthonormal(): lower = jnp.linalg.cholesky(gram)  15.2 us
  transfers between devices with their start and end apart: 4, of which 4 were waited for; matrix products, arithmetic and copies ran while one was open for 0% of the time, Pallas kernels for 0%

commit v1 on v0

--- a/solution.py
+++ b/solution.py
@@ -20,7 +20,8 @@
         partial_value.shape[0], partial_value.shape[1] * partial_value.shape[2]
     )
     shares = lax.psum_scatter(flat, ("wide", "narrow"), scatter_dimension=1, tiled=True)
-    whole = lax.all_gather(shares, ("wide", "narrow"), axis=1, tiled=True)
+    row_out = jax.lax.all_gather(shares, ("wide", "narrow"))
+    whole = jnp.concatenate(row_out, axis=1)
     return whole.reshape(partial_value.shape)
 
 

time: 506 us -> 504 us (level)
    unnamed x24 -> x22, local copies, waits for them, and re-layouts: 12.9 us -> 10.6 us
where the time goes in v1:
time: 504 us; the launch traced here: 503 us
  waiting for transfers between devices  235 us (47%)
  blocking collectives  180 us (36%)
  matrix products  30.3 us (6%)
  other arithmetic  28.2 us (6%)
  local copies, waits for them, and re-layouts  15.9 us (3%)
  between operations  14.1 us (3%)
    unnamed x7, waiting for transfers between devices  167 us
    reduce_scatter x1, waiting for transfers between devices, on_device(): lax.psum_scatter(unfold_part, 'wide', scatter_dimension=1, tiled=True)  67.9 us
    psum x1, blocking collectives, on_device(): lax.psum(contract('kaj,kab->jb', along_one, spread_two), ('wide', 'narrow'))  57.9 us
    all_gather x2, blocking collectives, full_core(): row_out = jax.lax.all_gather(shares, ('wide', 'narrow'))  43.6 us
    psum x1, blocking collectives, on_device(): lax.psum(jnp.dot(unfold_rows, weights_one, precision=highest), 'wide')  34.9 us
    psum x1, blocking collectives, on_device(): lax.psum(jnp.dot(product_three.T, product_three, precision=highest), 'wide')  33 us
    dot_general x12, matrix products, contract(): return jnp.einsum(form, left, right, precision=highest)  26.7 us
    another operation x9, other arithmetic, orthonormal(): lower = jnp.linalg.cholesky(gram)  15.2 us
  transfers between devices with their start and end apart: 4, of which 4 were waited for; matrix products, arithmetic and copies ran while one was open for 0% of the time, Pallas kernels for 0%

profile of v1, /device:TPU:0, one launch (start us, length us, event | category | flops | bytes accessed | tf_op | source)
XLA Modules:
  0.0 503.0 jit_solution(2988590821013599557)
XLA Ops:
  7.2 0.0 reduce-scatter.11.cloned.1.call-start
  7.2 1.3 copy-done
  8.6 3.1 fusion.12
  11.7 2.2 fusion.3
  13.9 0.0 reduce-scatter.11.cloned.1.call-update
  13.9 0.0 reduce-scatter.13.cloned.1.call-start
  13.9 67.9 %reduce-scatter.11.cloned.1.call-done = f32[64,288]{0,1:T(8,128)} async-done(((f32[64,2304]{0,1:T(8,128)}), f32[64,288]{0,1:T(8,128)}) %reduce-scatter.11.cloned.1.call-update) | async-done | bytes 73744 | tf_op jit(solution)/shard_map/reduce_scatter | solution.py:34
  81.9 1.2 fusion.34
  83.1 3.5 psum.42
  86.6 1.1 fusion.35
  87.7 34.9 %psum.43 = f32[64,48]{0,1:T(8,128)S(1)} all-reduce(f32[64,48]{0,1:T(8,128)S(1)} %fusion.35), channel_id=1, replica_groups=mesh['win'=2,'wide'=8,'narrow'=2] {'wide'}, use_global_device_ids=true, to_apply=%region_2.0 | all-reduce | flops 3072 | bytes 24576 | tf_op jit(solution)/shard_map/psum | solution.py:36
  122.6 0.2 fusion.36
  122.8 3.4 psum.44
  126.2 0.1 copy.41
  126.3 4.4 cholesky.59
  130.7 0.6 compare_reduce_fusion.2
  131.4 0.7 fusion.14
  132.0 3.7 custom-call.11
  135.7 0.2 fusion.25
  136.0 1.1 convolution_bitcast_fusion
  137.1 1.6 fusion
  138.7 3.1 fusion.31
  141.8 2.7 copy.60
  144.5 0.0 reduce-scatter.15.cloned.1.call-start
  144.6 55.5 %reduce-scatter.13.cloned.1.call-done = f32[144,48]{1,0:T(8,128)} async-done(((f32[2304,48]{1,0:T(8,128)}), f32[144,48]{1,0:T(8,128)}) %reduce-scatter.13.cloned.1.call-update) | async-done | bytes 27664
  200.1 1.0 copy.55
  201.0 21.8 %all-gather = f32[768,144]{1,0:T(8,128)S(1)} all-gather(f32[48,144]{1,0:T(8,128)S(1)} %copy.55), channel_id=2, replica_groups=mesh['win'=2,'wide'=8,'narrow'=2] {'wide','narrow'}, dimensions={0}, use_global_device_ids=true | all-gather | bytes 470016 | tf_op jit(solution)/shard_map/all_gather | solution.py:23
  222.8 0.5 copy.43
  223.3 1.6 reshape_reshape.6
  224.9 4.7 convolution_bitcast_fusion.3
  229.6 1.2 convolution_bitcast_fusion.4
  230.8 57.9 %psum.45 = f32[256,48]{0,1:T(8,128)S(1)} all-reduce(f32[256,48]{0,1:T(8,128)S(1)} %convolution_bitcast_fusion.4), channel_id=1, replica_groups=mesh['win'=2,'wide'=8,'narrow'=2] {'wide','narrow'}, use_global_device_ids=true, to_apply=%region_7.0 | all-reduce | flops 12288 | bytes 98304 | tf_op jit(solution)/shard_map/psum | solution.py:44
  288.7 0.2 fusion.37
  288.9 0.1 copy.45
  289.0 4.4 cholesky.70
  293.4 0.6 compare_reduce_fusion.1
  294.0 0.7 fusion.15
  294.7 3.7 custom-call.12
  298.4 0.2 fusion.20
  298.6 2.3 convolution_bitcast_fusion.2
  301.0 2.1 convolution_bitcast_fusion.1
  303.1 2.0 fusion.7
  305.2 1.5 copy.61
  306.7 0.0 reduce-scatter.17.cloned.1.call-start
  306.7 55.5 %reduce-scatter.15.cloned.1.call-done = f32[144,48]{1,0:T(8,128)} async-done(((f32[2304,48]{1,0:T(8,128)}), f32[144,48]{1,0:T(8,128)}) %reduce-scatter.15.cloned.1.call-update) | async-done | bytes 27664
  362.3 1.0 copy.57
  363.3 21.8 %all-gather.1 = f32[768,144]{1,0:T(8,128)S(1)} all-gather(f32[48,144]{1,0:T(8,128)S(1)} %copy.57), channel_id=3, replica_groups=mesh['win'=2,'wide'=8,'narrow'=2] {'wide','narrow'}, dimensions={0}, use_global_device_ids=true | all-gather | bytes 470016 | tf_op jit(solution)/shard_map/all_gather | solution.py:23
  385.0 1.3 copy.76
  386.4 1.7 reshape_reshape.7
  388.1 1.2 convolution_bitcast_fusion.5
  389.3 3.5 psum.46
  392.8 0.2 fusion.38
  393.0 33.0 %psum.47 = f32[48,48]{0,1:T(8,128)S(1)} all-reduce(f32[48,48]{0,1:T(8,128)S(1)} %fusion.38), channel_id=1, replica_groups=mesh['win'=2,'wide'=8,'narrow'=2] {'wide'}, use_global_device_ids=true, to_apply=%region_10.12 | all-reduce | flops 2304 | bytes 18432 | tf_op jit(solution)/shard_map/psum | solution.py:50
  426.1 0.1 copy.50
  426.1 4.4 cholesky.81
  430.6 0.6 compare_reduce_fusion
  431.2 0.7 fusion.16
  431.9 3.7 custom-call.13
  435.5 0.2 fusion.17
  435.7 2.0 fusion.5
  437.8 1.5 copy.62
  439.3 0.0 reduce-scatter.17.cloned.1.call-update
  439.3 55.6 %reduce-scatter.17.cloned.1.call-done = f32[144,48]{1,0:T(8,128)} async-done(((f32[2304,48]{1,0:T(8,128)}), f32[144,48]{1,0:T(8,128)}) %reduce-scatter.17.cloned.1.call-update) | async-done | bytes 27664
  494.9 1.6 copy.59
  (23 shorter events, 0.2 us)
Async XLA Ops:
  7.2 1.4 copy-start
  7.2 4.5 copy-start.3
  7.2 74.7 %reduce-scatter.11.cloned.1.call-start = ((), (), s32[]{:S(2)}) async-start(), calls=%async_computation.4 | async-start | bytes 1327104 | tf_op jit(solution)/shard_map/reduce_scatter | solution.py:34
  11.7 70.2 %copy-start.7 = (f32[64,48]{0,1:T(8,128)S(1)}, f32[64,48]{0,1:T(8,128)}, u32[]{:S(2)}) copy-start(f32[64,48]{0,1:T(8,128)} %param.6) | copy-start | bytes 36868
  13.9 186.2 %reduce-scatter.13.cloned.1.call-start = ((), (), s32[]{:S(2)}) async-start(), calls=%async_computation.5 | async-start | bytes 1253376
  135.9 1.1 copy-start.1
  136.0 1.1 copy-start.5
  144.5 217.7 %reduce-scatter.15.cloned.1.call-start = ((), (), s32[]{:S(2)}) async-start(), calls=%async_computation.6 | async-start | bytes 1253376
  294.7 6.3 %copy-start.2 = (f32[64,48]{0,1:T(8,128)S(1)}, f32[64,48]{0,1:T(8,128)}, u32[]{:S(2)}) copy-start(f32[64,48]{0,1:T(8,128)} %copy-done.1) | copy-start | bytes 36868
  298.6 4.5 copy-start.4
  306.7 188.2 %reduce-scatter.17.cloned.1.call-start = ((), (), s32[]{:S(2)}) async-start(), calls=%async_computation.7 | async-start | bytes 1253376
  435.7 3.6 copy-start.6
Sparse Core Ops, SparseCore 0:
  14.0 67.8 reduce-scatter.10
  144.7 55.3 reduce-scatter.12
  306.8 55.4 reduce-scatter.14
  439.4 55.3 reduce-scatter.16

commit v2 on v0

--- a/solution.py
+++ b/solution.py
@@ -40,7 +40,9 @@
         contract("kab,kc->abc", contract("kaj,jb->kab", along_one, factor_two), factor_three)
     )
     spread_two = contract("abc,kc->kab", core_two, factor_three)
-    product_two = lax.psum(contract("kaj,kab->jb", along_one, spread_two), ("wide", "narrow"))
+    block = contract("kaj,kab->jb", along_one, spread_two)
+    parts = lax.all_gather(block, ("wide", "narrow"), axis=0, tiled=False)
+    product_two = parts.sum(axis=0)
     basis_two = orthonormal(product_two, jnp.dot(product_two.T, product_two, precision=highest))
     along_new = contract("kij,jb->kib", window_data, basis_two)
     unfold_three = contract("kib,ia->kab", along_new, basis_one)

time: 506 us -> 470 us (0.929)
  blocking collectives: 180 us -> 141 us
    psum x1 -> x0, blocking collectives: 57.9 us -> none  [on_device(): lax.psum(contract('kaj,kab->jb', along_one, spread_two), ('wide', 'narrow'))]
    all_gather x0 -> x1, blocking collectives: none -> 19.6 us  [on_device(): parts = lax.all_gather(block, ('wide', 'narrow'), axis=0, tiled=False)]
    unnamed x24 -> x25, local copies, waits for them, and re-layouts: 12.9 us -> 13.1 us
where the time goes in v2:
time: 470 us; the launch traced here: 469 us
  waiting for transfers between devices  236 us (50%)
  blocking collectives  141 us (30%)
  matrix products  30.3 us (6%)
  other arithmetic  28.3 us (6%)
  local copies, waits for them, and re-layouts  18.8 us (4%)
  between operations  14.1 us (3%)
    unnamed x7, waiting for transfers between devices  168 us
    reduce_scatter x1, waiting for transfers between devices, on_device(): lax.psum_scatter(unfold_part, 'wide', scatter_dimension=1, tiled=True)  67.9 us
    all_gather x2, blocking collectives, full_core(): whole = lax.all_gather(shares, ('wide', 'narrow'), axis=1, tiled=True)  43.4 us
    psum x1, blocking collectives, on_device(): lax.psum(jnp.dot(unfold_rows, weights_one, precision=highest), 'wide')  34.9 us
    psum x1, blocking collectives, on_device(): lax.psum(jnp.dot(product_three.T, product_three, precision=highest), 'wide')  33.3 us
    dot_general x12, matrix products, contract(): return jnp.einsum(form, left, right, precision=highest)  26.7 us
    all_gather x1, blocking collectives, on_device(): parts = lax.all_gather(block, ('wide', 'narrow'), axis=0, tiled=False)  19.6 us
    another operation x9, other arithmetic, orthonormal(): lower = jnp.linalg.cholesky(gram)  15.2 us
  transfers between devices with their start and end apart: 4, of which 4 were waited for; matrix products, arithmetic and copies ran while one was open for 0% of the time, Pallas kernels for 0%

profile of v2, /device:TPU:0, one launch (start us, length us, event | category | flops | bytes accessed | tf_op | source)
XLA Modules:
  0.0 469.4 jit_solution(1440078477972940593)
XLA Ops:
  7.2 1.3 copy-done
  8.6 3.1 fusion.12
  11.7 2.2 fusion.3
  13.9 67.9 %reduce-scatter.11.cloned.1.call-done = f32[64,288]{0,1:T(8,128)} async-done(((f32[64,2304]{0,1:T(8,128)}), f32[64,288]{0,1:T(8,128)}) %reduce-scatter.11.cloned.1.call-update) | async-done | bytes 73744 | tf_op jit(solution)/shard_map/reduce_scatter | solution.py:33
  81.9 1.2 fusion.34
  83.1 3.5 psum.35
  86.6 1.1 fusion.35
  87.7 34.9 %psum.36 = f32[64,48]{0,1:T(8,128)S(1)} all-reduce(f32[64,48]{0,1:T(8,128)S(1)} %fusion.35), channel_id=1, replica_groups=mesh['win'=2,'wide'=8,'narrow'=2] {'wide'}, use_global_device_ids=true, to_apply=%region_2.0 | all-reduce | flops 3072 | bytes 24576 | tf_op jit(solution)/shard_map/psum | solution.py:35
  122.6 0.2 fusion.36
  122.8 3.4 psum.37
  126.2 0.1 copy.26
  126.3 4.4 cholesky.59
  130.7 0.6 compare_reduce_fusion.2
  131.4 0.7 fusion.14
  132.0 3.7 custom-call.11
  135.7 0.2 fusion.25
  136.0 1.1 convolution_bitcast_fusion
  137.1 1.6 fusion
  138.7 3.1 fusion.31
  141.8 2.7 copy.45
  144.5 0.0 reduce-scatter.15.cloned.1.call-start
  144.6 55.5 %reduce-scatter.13.cloned.1.call-done = f32[144,48]{1,0:T(8,128)} async-done(((f32[2304,48]{1,0:T(8,128)}), f32[144,48]{1,0:T(8,128)}) %reduce-scatter.13.cloned.1.call-update) | async-done | bytes 27664
  200.1 1.0 copy.40
  201.0 21.8 %all-gather.1 = f32[16,144,48]{1,2,0:T(8,128)S(1)} all-gather(f32[1,144,48]{1,2,0:T(8,128)S(1)} %bitcast.122), channel_id=1, replica_groups=mesh['win'=2,'wide'=8,'narrow'=2] {'wide','narrow'}, dimensions={0}, use_global_device_ids=true | all-gather | bytes 470016 | tf_op jit(solution)/shard_map/all_gather | solution.py:23
  222.8 0.5 copy.28
  223.3 1.2 reshape.48
  224.4 2.7 reshape.42
  227.2 4.7 %convolution_bitcast_fusion.3 = f32[24,48,48]{2,0,1:T(8,128)S(1)} fusion(f32[48,48,48]{2,1,0:T(8,128)} %reshape.42, f32[24,48]{1,0:T(8,128)S(1)} %copy-done.3), kind=kOutput, calls=%fused_computation.3 | convolution fusion | flops 31850496 | bytes 668160 | tf_op jit(solution)/shard_map/abc,kc->kab/dot_general | solution.py:10
  231.9 1.2 convolution_bitcast_fusion.4
  233.1 19.6 %all-gather = f32[4096,48]{0,1:T(8,128)S(1)} all-gather(f32[256,48]{0,1:T(8,128)S(1)} %convolution_bitcast_fusion.4), channel_id=2, replica_groups=mesh['win'=2,'wide'=8,'narrow'=2] {'wide','narrow'}, dimensions={0}, use_global_device_ids=true | all-gather | bytes 835584 | tf_op jit(solution)/shard_map/all_gather | solution.py:44
  252.7 0.2 copy.48
  253.0 0.1 bitcast_reduce_fusion
  253.1 0.2 fusion.37
  253.3 0.1 copy.30
  253.4 4.4 cholesky.70
  257.8 0.6 compare_reduce_fusion.1
  258.4 0.7 fusion.15
  259.1 3.7 custom-call.12
  262.8 0.3 fusion.20
  263.0 2.3 convolution_bitcast_fusion.2
  265.4 2.1 convolution_bitcast_fusion.1
  267.5 2.0 fusion.7
  269.6 1.5 copy.46
  271.1 0.0 reduce-scatter.17.cloned.1.call-start
  271.1 57.4 %reduce-scatter.15.cloned.1.call-done = f32[144,48]{1,0:T(8,128)} async-done(((f32[2304,48]{1,0:T(8,128)}), f32[144,48]{1,0:T(8,128)}) %reduce-scatter.15.cloned.1.call-update) | async-done | bytes 27664
  328.5 1.0 copy.42
  329.5 21.6 %all-gather.2 = f32[16,144,48]{1,2,0:T(8,128)S(1)} all-gather(f32[1,144,48]{1,2,0:T(8,128)S(1)} %bitcast.123), channel_id=1, replica_groups=mesh['win'=2,'wide'=8,'narrow'=2] {'wide','narrow'}, dimensions={0}, use_global_device_ids=true | all-gather | bytes 470016 | tf_op jit(solution)/shard_map/all_gather | solution.py:23
  351.0 0.5 copy.32
  351.5 1.1 reshape.50
  352.7 1.7 reshape.44
  354.4 1.2 convolution_bitcast_fusion.5
  355.6 3.5 psum.38
  359.1 0.2 fusion.38
  359.3 33.3 %psum.39 = f32[48,48]{0,1:T(8,128)S(1)} all-reduce(f32[48,48]{0,1:T(8,128)S(1)} %fusion.38), channel_id=1, replica_groups=mesh['win'=2,'wide'=8,'narrow'=2] {'wide'}, use_global_device_ids=true, to_apply=%region_10.12 | all-reduce | flops 2304 | bytes 18432 | tf_op jit(solution)/shard_map/psum | solution.py:51
  392.6 0.1 copy.35
  392.7 4.4 cholesky.81
  397.1 0.6 compare_reduce_fusion
  397.7 0.7 fusion.16
  398.4 3.7 custom-call.13
  402.1 0.2 fusion.17
  402.3 2.0 fusion.5
  404.3 1.5 copy.47
  405.8 55.5 %reduce-scatter.17.cloned.1.call-done = f32[144,48]{1,0:T(8,128)} async-done(((f32[2304,48]{1,0:T(8,128)}), f32[144,48]{1,0:T(8,128)}) %reduce-scatter.17.cloned.1.call-update) | async-done | bytes 27664
  461.3 1.6 copy.44
  (27 shorter events, 0.3 us)
Async XLA Ops:
  7.2 1.4 copy-start
  7.2 4.5 copy-start.3
  7.2 74.7 %reduce-scatter.11.cloned.1.call-start = ((), (), s32[]{:S(2)}) async-start(), calls=%async_computation.4 | async-start | bytes 1327104 | tf_op jit(solution)/shard_map/reduce_scatter | solution.py:33
  11.7 70.2 %copy-start.7 = (f32[64,48]{0,1:T(8,128)S(1)}, f32[64,48]{0,1:T(8,128)}, u32[]{:S(2)}) copy-start(f32[64,48]{0,1:T(8,128)} %param.6) | copy-start | bytes 36868
  13.9 186.2 %reduce-scatter.13.cloned.1.call-start = ((), (), s32[]{:S(2)}) async-start(), calls=%async_computation.5 | async-start | bytes 1253376
  135.9 1.1 copy-start.1
  136.0 1.1 copy-start.5
  144.5 184.0 %reduce-scatter.15.cloned.1.call-start = ((), (), s32[]{:S(2)}) async-start(), calls=%async_computation.6 | async-start | bytes 1253376
  259.1 6.3 %copy-start.2 = (f32[64,48]{0,1:T(8,128)S(1)}, f32[64,48]{0,1:T(8,128)}, u32[]{:S(2)}) copy-start(f32[64,48]{0,1:T(8,128)} %copy-done.1) | copy-start | bytes 36868
  263.0 4.5 copy-start.4
  271.1 190.2 %reduce-scatter.17.cloned.1.call-start = ((), (), s32[]{:S(2)}) async-start(), calls=%async_computation.7 | async-start | bytes 1253376
  402.2 3.6 copy-start.6
Sparse Core Ops, SparseCore 0:
  14.0 67.8 reduce-scatter.10
  144.7 55.3 reduce-scatter.12
  271.2 57.2 reduce-scatter.14
  405.9 55.3 reduce-scatter.16
